TPU v7x, 256 devices: a whole 4x4x8 slice. The times are simulated.
256 devices in a mesh: segment: 4 (over y), mp: 16 (over z, core), dp: 4 (over x).
Axes of the slice: x: 4, y: 4, z: 8, core: 2. Of those that a mesh axis runs over, the one named last changes fastest.
Arguments:
- text_rows: bfloat16 [4, 512, 1024], P(None, 'dp'), may hold values from -6 to 6
- durations: int32 [4, 4, 128], P(None, 'dp'), may hold values from 1 to 16, 512 in all within a row
- unit_targets: int32 [4, 2048], P(None, 'dp'), may hold values from 0 to 9999
- w_in: bfloat16 [4, 1024, 8192], P('segment', None, 'mp'), may hold values from -0.1875 to 0.1875
- w_out: bfloat16 [4, 8192, 1024], P('segment', 'mp'), may hold values from -0.0625 to 0.0625
- w_unit: bfloat16 [1024, 10240], P(None, ('segment', 'mp')), as said below
Outputs:
- loss: float32 [4], P('dp')
- grad_in: float32 [4, 1024, 8192], P('segment', 'dp', 'mp')
- grad_out: float32 [4, 8192, 1024], P('segment', 'mp', 'dp')
- grad_unit: float32 [1024, 10240], P('dp', ('segment', 'mp'))
Inputs may be any that keep to these rules, and one draw needn't show every extreme that they name: Within each micro-batch and each index of dp the 128 durations sum to exactly 512, and one of them equals 16. `w_unit`: entries of order 3 / sqrt(1024) in most columns, some columns much larger.
All inputs are finite; a program needn't handle non-finite values.
Results may differ from a plain program's by a relative error of at most 0.035.
Values may be sent and summed in bfloat16 or wider, within the bound.
A program may use at most 128 MiB of HBM per device.

v0:
```python
import jax
import jax.numpy as jnp
from jax import lax
from jax.sharding import PartitionSpec as P


def shifted(block, axis, distance):
    devices = range(lax.axis_size(axis))
    route = [(i - distance, i) for i in devices if i - distance in devices]
    return lax.ppermute(block, axis, route)


def broadcast(x, axis, root):
    mine = lax.axis_index(axis) == root
    return lax.psum(jnp.where(mine, x, jnp.zeros_like(x)), axis)


def gelu_parts(pre_vals):
    coeff = 0.7978845608
    inner = coeff * (pre_vals + 0.044715 * pre_vals * pre_vals * pre_vals)
    tanh_val = jnp.tanh(inner)
    value = 0.5 * pre_vals * (1.0 + tanh_val)
    slope = 0.5 * (1.0 + tanh_val) + 0.5 * pre_vals * (1.0 - tanh_val * tanh_val) * coeff * (
        1.0 + 3.0 * 0.044715 * pre_vals * pre_vals
    )
    return (value, slope)


def row_scale(rows_in):
    floats = rows_in.astype(jnp.float32)
    return lax.rsqrt(jnp.mean(floats * floats, axis=-1, keepdims=True) + 1e-06)


def norm_back(rows_in, grads):
    scale = row_scale(rows_in)
    normal = rows_in.astype(jnp.float32) * scale
    return scale * (grads - normal * jnp.mean(grads * normal, axis=-1, keepdims=True))


def section(rows_in, first):
    normed = (rows_in.astype(jnp.float32) * row_scale(rows_in)).astype(jnp.bfloat16)
    pre_vals = jnp.dot(normed, first, preferred_element_type=jnp.float32)
    value, slope = gelu_parts(pre_vals)
    return (normed, value.astype(jnp.bfloat16), slope)


def finish_forward(pieces, summed):
    return (pieces[0].astype(jnp.float32) + summed).astype(jnp.bfloat16)


def finish_backward(pieces, summed):
    return (pieces[0].astype(jnp.float32) + norm_back(pieces[1], summed)).astype(jnp.bfloat16)


def reduce_rows(partial_value, pieces, finisher):
    summed = lax.psum(partial_value, "mp")
    return finisher(pieces, summed)


def on_device(text_rows, durations, unit_targets, w_in, w_out, w_unit):
    micro_count, row_count, width = text_rows.shape
    segments = lax.axis_size("segment")
    segment_at = lax.axis_index("segment")
    first = w_in[0]
    second = w_out[0]
    clocks = micro_count + segments - 1
    stash = jnp.zeros((micro_count, row_count, width), jnp.bfloat16)
    final_rows = jnp.zeros((micro_count, row_count, width), jnp.bfloat16)
    outgoing = jnp.zeros((row_count, width), jnp.bfloat16)
    for clock in range(clocks):
        if clock > 0:
            incoming = shifted(outgoing, "segment", 1)
        else:
            incoming = jnp.zeros((row_count, width), jnp.bfloat16)
        rows_in = jnp.where(segment_at == 0, text_rows[min(clock, micro_count - 1)], incoming)
        batch_at = clock - segment_at
        is_live = (batch_at >= 0) & (batch_at < micro_count)
        slot_at = jnp.clip(batch_at, 0, micro_count - 1)
        stash = jnp.where(
            is_live, lax.dynamic_update_index_in_dim(stash, rows_in, slot_at, 0), stash
        )
        normed, hidden, slope = section(rows_in, first)
        partial_value = jnp.dot(hidden, second, preferred_element_type=jnp.float32)
        outgoing = reduce_rows(partial_value, (rows_in,), finish_forward)
        is_last = is_live & (segment_at == segments - 1)
        final_rows = jnp.where(
            is_last, lax.dynamic_update_index_in_dim(final_rows, outgoing, slot_at, 0), final_rows
        )
    final_rows = broadcast(final_rows, "segment", segments - 1)
    vocab_part = w_unit.shape[1]
    vocab_start = lax.axis_index(("segment", "mp")) * vocab_part
    final_norm = (final_rows.astype(jnp.float32) * row_scale(final_rows)).astype(jnp.bfloat16)
    logits = jnp.einsum("mrd,dv->mrv", final_norm, w_unit, preferred_element_type=jnp.float32)
    lengths = durations[:, 0, :]
    unit_count = unit_targets.shape[1]
    ends = jnp.cumsum(lengths, axis=-1)
    positions = jnp.arange(unit_count, dtype=jnp.int32)
    row_local = jnp.sum((ends[:, None, :] <= positions[None, :, None]).astype(jnp.int32), axis=-1)
    row_onehot = (
        row_local[:, :, None] == jnp.arange(row_count, dtype=jnp.int32)[None, None, :]
    ).astype(jnp.bfloat16)
    vocab_ids = vocab_start + jnp.arange(vocab_part, dtype=jnp.int32)
    target_hits = (unit_targets[:, :, None] == vocab_ids[None, None, :]).astype(jnp.bfloat16)
    counts = jnp.einsum("mur,muv->mrv", row_onehot, target_hits, preferred_element_type=jnp.float32)
    local_peak = jnp.max(logits, axis=-1)
    target_local = jnp.sum(counts * logits, axis=-1)
    peak = lax.pmax(local_peak, ("segment", "mp"))
    total, target_sum = lax.psum(
        (jnp.sum(jnp.exp(logits - peak[..., None]), axis=-1), target_local), ("segment", "mp")
    )
    lse = peak + jnp.log(total)
    denom = float(micro_count * unit_count * lax.axis_size("dp"))
    length_f = lengths.astype(jnp.float32)
    loss_local = jnp.sum(length_f * lse - target_sum)
    loss = (loss_local / denom)[None]
    dlogits = ((length_f[..., None] * jnp.exp(logits - lse[..., None]) - counts) / denom).astype(
        jnp.bfloat16
    )
    grad_unit = jnp.einsum("mrd,mrv->dv", final_norm, dlogits, preferred_element_type=jnp.float32)
    norm_part = jnp.einsum("mrv,dv->mrd", dlogits, w_unit, preferred_element_type=jnp.float32)
    norm_share = lax.psum_scatter(
        norm_part, ("segment", "mp"), scatter_dimension=2, tiled=True
    ).astype(jnp.bfloat16)
    dnorm = lax.all_gather(norm_share, ("segment", "mp"), axis=2, tiled=True)
    grad_final = norm_back(final_rows, dnorm.astype(jnp.float32)).astype(jnp.bfloat16)
    grad_first = jnp.zeros(first.shape, jnp.float32)
    grad_second = jnp.zeros(second.shape, jnp.float32)
    going_back = jnp.zeros((row_count, width), jnp.bfloat16)
    for clock in range(clocks):
        if clock > 0:
            arriving = shifted(going_back, "segment", -1)
        else:
            arriving = jnp.zeros((row_count, width), jnp.bfloat16)
        grad_rows = jnp.where(
            segment_at == segments - 1, grad_final[min(clock, micro_count - 1)], arriving
        )
        batch_at = clock - (segments - 1 - segment_at)
        is_live = (batch_at >= 0) & (batch_at < micro_count)
        slot_at = jnp.clip(batch_at, 0, micro_count - 1)
        rows_in = lax.dynamic_index_in_dim(stash, slot_at, 0, keepdims=False)
        normed, hidden, slope = section(rows_in, first)
        live_f = is_live.astype(jnp.float32)
        grad_second = grad_second + live_f * jnp.dot(
            hidden.T, grad_rows, preferred_element_type=jnp.float32
        )
        dhidden = jnp.dot(grad_rows, second.T, preferred_element_type=jnp.float32)
        dpre = (dhidden * slope).astype(jnp.bfloat16)
        grad_first = grad_first + live_f * jnp.dot(
            normed.T, dpre, preferred_element_type=jnp.float32
        )
        dnormed = jnp.dot(dpre, first.T, preferred_element_type=jnp.float32)
        going_back = reduce_rows(dnormed, (grad_rows, rows_in), finish_backward)
    sum_first, sum_second, sum_unit = (
        lax.psum_scatter(grad_first, "dp", scatter_dimension=0, tiled=True),
        lax.psum_scatter(grad_second, "dp", scatter_dimension=1, tiled=True),
        lax.psum_scatter(grad_unit, "dp", scatter_dimension=0, tiled=True),
    )
    return (loss, sum_first[None], sum_second[None], sum_unit)


def solution(mesh):
    placed = (
        P(None, "dp", None),
        P(None, "dp", None),
        P(None, "dp"),
        P("segment", None, "mp"),
        P("segment", "mp", None),
        P(None, ("segment", "mp")),
    )
    return jax.shard_map(
        on_device,
        mesh=mesh,
        in_specs=placed,
        out_specs=(
            P("dp"),
            P("segment", "dp", "mp"),
            P("segment", "mp", "dp"),
            P("dp", ("segment", "mp")),
        ),
        check_vma=False,
    )
```

profile of v0, /device:TPU:1, one launch (start us, length us, event | category | flops | bytes accessed | tf_op | source)
XLA Modules:
  0.0 2379.7 jit_solution(6565013018614124377)
XLA Ops:
  8.5 2.7 fusion.35
  11.3 113.5 %all-reduce.18.cloned.1.call-done = f32[128,1024]{1,0:T(8,128)} async-done(((f32[128,1024]{1,0:T(8,128)}), f32[128,1024]{1,0:T(8,128)}) %all-reduce.18.cloned.1.call-update) | async-done | bytes 524304 | tf_op jit(solution)/shard_map/psum | solution.py:56
  126.2 3.8 collective-permute-start
  131.2 3.0 collective-permute-done
  137.0 111.0 %all-reduce.20.cloned.1.call-done = f32[128,1024]{1,0:T(8,128)} async-done(((f32[128,1024]{1,0:T(8,128)}), f32[128,1024]{1,0:T(8,128)}) %all-reduce.20.cloned.1.call-update) | async-done | bytes 524304 | tf_op jit(solution)/shard_map/psum | solution.py:56
  248.0 2.0 fusion.308
  250.1 3.1 collective-permute-start.1
  253.2 5.2 collective-permute-done.1
  261.9 110.8 %all-reduce.22.cloned.1.call-done = f32[128,1024]{1,0:T(8,128)} async-done(((f32[128,1024]{1,0:T(8,128)}), f32[128,1024]{1,0:T(8,128)}) %all-reduce.22.cloned.1.call-update) | async-done | bytes 524304 | tf_op jit(solution)/shard_map/psum | solution.py:56
  372.6 2.0 fusion.307
  374.7 3.1 collective-permute-start.2
  377.8 5.2 collective-permute-done.2
  386.5 110.8 %all-reduce.24.cloned.1.call-done = f32[128,1024]{1,0:T(8,128)} async-done(((f32[128,1024]{1,0:T(8,128)}), f32[128,1024]{1,0:T(8,128)}) %all-reduce.24.cloned.1.call-update) | async-done | bytes 524304 | tf_op jit(solution)/shard_map/psum | solution.py:56
  497.3 2.0 fusion.306
  499.3 3.1 collective-permute-start.3
  502.4 5.2 collective-permute-done.3
  511.1 110.8 %all-reduce.26.cloned.1.call-done = f32[128,1024]{1,0:T(8,128)} async-done(((f32[128,1024]{1,0:T(8,128)}), f32[128,1024]{1,0:T(8,128)}) %all-reduce.26.cloned.1.call-update) | async-done | bytes 524304 | tf_op jit(solution)/shard_map/psum | solution.py:56
  621.9 2.0 fusion.305
  623.9 3.1 collective-permute-start.4
  627.0 5.2 collective-permute-done.4
  635.7 110.8 %all-reduce.28.cloned.1.call-done = f32[128,1024]{1,0:T(8,128)} async-done(((f32[128,1024]{1,0:T(8,128)}), f32[128,1024]{1,0:T(8,128)}) %all-reduce.28.cloned.1.call-update) | async-done | bytes 524304 | tf_op jit(solution)/shard_map/psum | solution.py:56
  746.5 2.0 fusion.304
  748.5 3.1 collective-permute-start.5
  751.7 5.2 collective-permute-done.5
  760.3 110.8 %all-reduce.30.cloned.1.call-done = f32[128,1024]{1,0:T(8,128)} async-done(((f32[128,1024]{1,0:T(8,128)}), f32[128,1024]{1,0:T(8,128)}) %all-reduce.30.cloned.1.call-update) | async-done | bytes 524304 | tf_op jit(solution)/shard_map/psum | solution.py:56
  871.1 2.0 fusion.259
  876.2 49.1 %all-reduce.32.cloned.1.call-done = bf16[4,128,1024]{2,1,0:T(8,128)(2,1)} async-done(((bf16[4,128,1024]{2,1,0:T(8,128)(2,1)}), bf16[4,128,1024]{2,1,0:T(8,128)(2,1)}) %all-reduce.32.cloned.1.call-update) | async-done | bytes 1048592 | tf_op jit(solution)/shard_map/psum | solution.py:15
  926.8 2.5 fusion.571
  929.3 125.5 %pmax.7 = f32[4,128]{1,0:T(4,128)S(1)} all-reduce(f32[4,128]{1,0:T(4,128)S(1)} %get-tuple-element.40), channel_id=1, replica_groups=mesh['segment'=4,'mp'=16,'dp'=4] {'segment','mp'}, use_global_device_ids=true, to_apply=%region_17.18 | all-reduce | flops 512 | bytes 4096 | tf_op jit(solution)/shard_map/pmax | solution.py:107
  1054.8 2.3 exponential_reduce_fusion
  1057.1 127.1 %psum.120 = f32[4,128]{1,0:T(4,128)S(1)} all-reduce(f32[4,128]{1,0:T(4,128)S(1)} %get-tuple-element.12), channel_id=1, replica_groups=mesh['segment'=4,'mp'=16,'dp'=4] {'segment','mp'}, use_global_device_ids=true, to_apply=%region_19.20 | all-reduce | flops 512 | bytes 4096 | tf_op jit(solution)/shard_map/psum | solution.py:108
  1186.5 2.7 copy.13
  1189.2 265.5 %all-reduce.45 = (f32[4,128]{1,0:T(4,128)}, bf16[4,128,1024]{1,0,2:T(4,128)(2,1)}) all-reduce(f32[4,128]{1,0:T(4,128)S(1)} %get-tuple-element.13, f32[4,128,1024]{1,0,2:T(4,128)} %copy.13), channel_id=1, replica_groups=mesh['segment'=4,'mp'=16,'dp'=4] {'segment','mp'}, use_global_device_ids=true, to_apply=%region_23.24 | all-reduce | flops 524800 | bytes 3149824 | tf_op jit(solution)/shard_map/psum | solution.py:108
  1456.9 75.1 %all-gather.2.cloned.1.call-done = bf16[4,128,1024]{1,0,2:T(4,128)(2,1)} async-done(((bf16[4,128,16]{1,0,2:T(4,128)(2,1)}), bf16[4,128,1024]{1,0,2:T(4,128)(2,1)}) %all-gather.2.cloned.1.call-update) | async-done | bytes 1048592 | tf_op jit(solution)/shard_map/all_gather | solution.py:124
  1531.9 2.5 copy.14
  1534.4 2.2 fusion.3
  1540.1 106.9 %all-reduce.34.cloned.1.call-done = f32[128,1024]{1,0:T(8,128)} async-done(((f32[128,1024]{1,0:T(8,128)}), f32[128,1024]{1,0:T(8,128)}) %all-reduce.34.cloned.1.call-update) | async-done | bytes 524304 | tf_op jit(solution)/shard_map/psum | solution.py:56
  1647.0 2.2 fusion.159
  1651.1 7.3 collective-permute-done.6
  1661.0 109.8 %all-reduce.36.cloned.1.call-done = f32[128,1024]{1,0:T(8,128)} async-done(((f32[128,1024]{1,0:T(8,128)}), f32[128,1024]{1,0:T(8,128)}) %all-reduce.36.cloned.1.call-update) | async-done | bytes 524304 | tf_op jit(solution)/shard_map/psum | solution.py:56
  1775.8 6.7 collective-permute-done.7
  1786.7 109.8 %all-reduce.38.cloned.1.call-done = f32[128,1024]{1,0:T(8,128)} async-done(((f32[128,1024]{1,0:T(8,128)}), f32[128,1024]{1,0:T(8,128)}) %all-reduce.38.cloned.1.call-update) | async-done | bytes 524304 | tf_op jit(solution)/shard_map/psum | solution.py:56
  1901.5 6.7 collective-permute-done.8
  1912.4 109.8 %all-reduce.40.cloned.1.call-done = f32[128,1024]{1,0:T(8,128)} async-done(((f32[128,1024]{1,0:T(8,128)}), f32[128,1024]{1,0:T(8,128)}) %all-reduce.40.cloned.1.call-update) | async-done | bytes 524304 | tf_op jit(solution)/shard_map/psum | solution.py:56
  2027.3 6.7 collective-permute-done.9
  2038.2 109.8 %all-reduce.42.cloned.1.call-done = f32[128,1024]{1,0:T(8,128)} async-done(((f32[128,1024]{1,0:T(8,128)}), f32[128,1024]{1,0:T(8,128)}) %all-reduce.42.cloned.1.call-update) | async-done | bytes 524304 | tf_op jit(solution)/shard_map/psum | solution.py:56
  2153.0 6.7 collective-permute-done.10
  2164.0 2.6 convolution_bitcast_fusion
  2166.9 2.9 fusion.403
  2169.9 1.8 fusion.418
  2173.5 1.8 fusion.420
  2175.3 1.9 fusion.421
  2178.9 94.8 %all-reduce.44.cloned.1.call-done = f32[128,1024]{1,0:T(8,128)} async-done(((f32[128,1024]{1,0:T(8,128)}), f32[128,1024]{1,0:T(8,128)}) %all-reduce.44.cloned.1.call-update) | async-done | bytes 524304 | tf_op jit(solution)/shard_map/psum | solution.py:56
  2278.2 7.3 collective-permute-done.11
  2286.2 6.7 multiply_add_fusion
  2293.0 2.6 fusion.283
  2295.6 1.8 fusion.285
  2297.5 1.9 fusion.287
  2299.3 1.9 fusion.289
  2301.2 1.9 fusion.291
  2303.1 1.9 fusion.293
  2305.0 7.7 multiply_add_fusion.1
  2314.6 21.9 reduce-scatter.6.cloned.1.call-done
  2336.6 35.2 %reduce-scatter.4.cloned.1.call-done = f32[256,512]{1,0:T(8,128)} async-done(((f32[1024,512]{1,0:T(8,128)}), f32[256,512]{1,0:T(8,128)}) %reduce-scatter.4.cloned.1.call-update) | async-done | bytes 524304 | tf_op jit(solution)/shard_map/reduce_scatter | solution.py:154
  (261 shorter events, 86.9 us)
Async XLA Ops:
  7.2 117.6 %all-reduce.18.cloned.1.call-start = ((), (), s32[]{:S(2)}) async-start(), calls=%async_computation.3 | async-start | bytes 1048576 | tf_op jit(solution)/shard_map/psum | solution.py:56
  11.2 236.8 %all-reduce.20.cloned.1.call-start = ((), (), s32[]{:S(2)}) async-start(), calls=%async_computation.4 | async-start | bytes 1048576 | tf_op jit(solution)/shard_map/psum | solution.py:56
  124.9 10.6 copy-start.1
  126.2 3.8 copy-start.3
  126.2 8.0 collective-permute-start
  137.0 235.7 %all-reduce.22.cloned.1.call-start = ((), (), s32[]{:S(2)}) async-start(), calls=%async_computation.5 | async-start | bytes 1048576 | tf_op jit(solution)/shard_map/psum | solution.py:56
  250.1 8.3 collective-permute-start.1
  261.8 235.4 %all-reduce.24.cloned.1.call-start = ((), (), s32[]{:S(2)}) async-start(), calls=%async_computation.6 | async-start | bytes 1048576 | tf_op jit(solution)/shard_map/psum | solution.py:56
  374.7 8.3 collective-permute-start.2
  386.4 235.4 %all-reduce.26.cloned.1.call-start = ((), (), s32[]{:S(2)}) async-start(), calls=%async_computation.7 | async-start | bytes 1048576 | tf_op jit(solution)/shard_map/psum | solution.py:56
  499.3 8.3 collective-permute-start.3
  511.0 235.4 %all-reduce.28.cloned.1.call-start = ((), (), s32[]{:S(2)}) async-start(), calls=%async_computation.8 | async-start | bytes 1048576 | tf_op jit(solution)/shard_map/psum | solution.py:56
  623.9 8.3 collective-permute-start.4
  635.7 235.4 %all-reduce.30.cloned.1.call-start = ((), (), s32[]{:S(2)}) async-start(), calls=%async_computation.9 | async-start | bytes 1048576 | tf_op jit(solution)/shard_map/psum | solution.py:56
  748.5 8.3 collective-permute-start.5
  760.3 165.0 %all-reduce.32.cloned.1.call-start = ((), (), s32[]{:S(2)}) async-start(), calls=%async_computation.10 | async-start | bytes 2097152 | tf_op jit(solution)/shard_map/psum | solution.py:15
  871.1 3.5 copy-start.60
  873.1 53.7 %copy-start.40 = (bf16[1024,160]{0,1:T(8,128)(2,1)S(1)}, bf16[1024,160]{0,1:T(8,128)(2,1)}, u32[]{:S(2)}) copy-start(bf16[1024,160]{0,1:T(8,128)(2,1)} %param.11) | copy-start | bytes 983044
  874.2 180.6 %copy-start.59 = (s32[4,512]{1,0:T(4,128)S(1)}, s32[4,512]{1,0:T(4,128)}, u32[]{:S(2)}) copy-start(s32[4,512]{1,0:T(4,128)} %param.8) | copy-start | bytes 24580
  874.2 657.7 %all-gather.2.cloned.1.call-start = ((), (), s32[]{:S(2)}) async-start(), calls=%async_computation.11 | async-start | bytes 1064960 | tf_op jit(solution)/shard_map/all_gather | solution.py:124
  1456.1 190.9 %all-reduce.34.cloned.1.call-start = ((), (), s32[]{:S(2)}) async-start(), calls=%async_computation.12 | async-start | bytes 1048576 | tf_op jit(solution)/shard_map/psum | solution.py:56
  1456.5 192.7 %copy-start.55 = (f32[128]{0:T(128)}, f32[128]{0:T(128)S(1)}, u32[]{:S(2)}) copy-start(f32[128]{0:T(128)S(1)} %add_rsqrt_fusion.7) | copy-start | bytes 1540
  1456.9 80.3 %copy-start.29 = (f32[128,512]{1,0:T(8,128)}, f32[128,512]{1,0:T(8,128)S(1)}, u32[]{:S(2)}) copy-start(f32[128,512]{1,0:T(8,128)S(1)} %fusion.61) | copy-start | bytes 786436
  1540.0 230.8 %all-reduce.36.cloned.1.call-start = ((), (), s32[]{:S(2)}) async-start(), calls=%async_computation.13 | async-start | bytes 1048576 | tf_op jit(solution)/shard_map/psum | solution.py:56
  1649.4 9.0 collective-permute-start.6
  1650.7 121.4 %copy-start.47 = (f32[128]{0:T(128)}, f32[128]{0:T(128)S(1)}, u32[]{:S(2)}) copy-start(f32[128]{0:T(128)S(1)} %add_rsqrt_fusion.6) | copy-start | bytes 1540
  1651.1 7.4 copy-start.19
  1661.0 235.5 %all-reduce.38.cloned.1.call-start = ((), (), s32[]{:S(2)}) async-start(), calls=%async_computation.14 | async-start | bytes 1048576 | tf_op jit(solution)/shard_map/psum | solution.py:56
  1773.4 9.0 collective-permute-start.7
  1775.4 122.4 %copy-start.49 = (f32[128]{0:T(128)}, f32[128]{0:T(128)S(1)}, u32[]{:S(2)}) copy-start(f32[128]{0:T(128)S(1)} %add_rsqrt_fusion.5) | copy-start | bytes 1540
  1775.7 8.9 copy-start.21
  1786.6 235.6 %all-reduce.40.cloned.1.call-start = ((), (), s32[]{:S(2)}) async-start(), calls=%async_computation.15 | async-start | bytes 1048576 | tf_op jit(solution)/shard_map/psum | solution.py:56
  1899.1 9.0 collective-permute-start.8
  1901.1 122.4 %copy-start.51 = (f32[128]{0:T(128)}, f32[128]{0:T(128)S(1)}, u32[]{:S(2)}) copy-start(f32[128]{0:T(128)S(1)} %add_rsqrt_fusion.4) | copy-start | bytes 1540
  1901.5 8.9 copy-start.23
  1912.4 235.6 %all-reduce.42.cloned.1.call-start = ((), (), s32[]{:S(2)}) async-start(), calls=%async_computation.16 | async-start | bytes 1048576 | tf_op jit(solution)/shard_map/psum | solution.py:56
  2024.9 9.0 collective-permute-start.9
  2026.9 122.4 %copy-start.53 = (f32[128]{0:T(128)}, f32[128]{0:T(128)S(1)}, u32[]{:S(2)}) copy-start(f32[128]{0:T(128)S(1)} %add_rsqrt_fusion.3) | copy-start | bytes 1540
  2027.2 8.9 copy-start.25
  2038.1 235.6 %all-reduce.44.cloned.1.call-start = ((), (), s32[]{:S(2)}) async-start(), calls=%async_computation.17 | async-start | bytes 1048576 | tf_op jit(solution)/shard_map/psum | solution.py:56
  2150.7 9.0 collective-permute-start.10
  2153.0 9.0 copy-start.27
  2163.9 150.7 %reduce-scatter.8.cloned.1.call-start = ((), (), s32[]{:S(2)}) async-start(), calls=%async_computation.20 | async-start | bytes 819200 | tf_op jit(solution)/shard_map/reduce_scatter | solution.py:156
  2166.6 169.9 %reduce-scatter.6.cloned.1.call-start = ((), (), s32[]{:S(2)}) async-start(), calls=%async_computation.19 | async-start | bytes 2621440 | tf_op jit(solution)/shard_map/reduce_scatter | solution.py:155
  2166.9 4.8 copy-start.9
  2166.9 4.8 copy-start.22
  2169.9 3.6 copy-start.11
  2169.9 3.6 copy-start.24
  2171.7 3.6 copy-start.13
  2171.7 3.6 copy-start.26
  2173.5 3.7 copy-start.15
  2173.5 3.7 copy-start.28
  2273.8 12.4 copy-start.7
  2276.5 9.0 collective-permute-start.11
  2277.8 15.1 copy-start.56
  2292.9 78.8 %reduce-scatter.4.cloned.1.call-start = ((), (), s32[]{:S(2)}) async-start(), calls=%async_computation.18 | async-start | bytes 2621440 | tf_op jit(solution)/shard_map/reduce_scatter | solution.py:154
  2293.0 4.5 copy-start.33
  2293.0 4.5 copy-start.50
  2295.6 3.7 copy-start.35
  2295.6 3.7 copy-start.52
  2297.5 3.8 copy-start.37
  2297.5 3.8 copy-start.54
  2299.3 3.8 copy-start.39
  2301.2 3.8 copy-start.57
  (27 other events, 34.2 us)
Sparse Core Ops, SparseCore 0:
  11.4 113.3 all-reduce.17
  137.1 110.8 all-reduce.19
  261.9 110.6 all-reduce.21
  386.5 110.6 all-reduce.23
  511.2 110.6 all-reduce.25
  635.8 110.6 all-reduce.27
  760.4 110.6 all-reduce.29
  874.3 50.9 all-reduce.31
  1456.2 75.6 all-gather.1
  1540.1 106.8 all-reduce.33
  1661.1 109.7 all-reduce.35
  1786.8 109.7 all-reduce.37
  1912.5 109.7 all-reduce.39
  2038.3 109.7 all-reduce.41
  2164.0 109.6 all-reduce.43
  2276.7 23.4 reduce-scatter.7
  2303.2 33.2 reduce-scatter.5
  2339.7 31.9 reduce-scatter.3
where the time goes:
time: 2380 us
  waiting for transfers between devices  1670 us (70%)
  blocking collectives  518 us (22%)
  matrix products  70.9 us (3%)
  other arithmetic  53.3 us (2%)
  starting transfers between devices  28.3 us (1%)
    psum x13, waiting for transfers between devices, reduce_rows(): summed = lax.psum(partial_value, 'mp')  1420 us
    psum x2, blocking collectives, on_device(): lax.psum((jnp.sum(jnp.exp(logits - peak[..., None]), axis=-1), target_loc...  393 us
    pmax x1, blocking collectives, on_device(): peak = lax.pmax(local_peak, ('segment', 'mp'))  125 us
    all_gather x1, waiting for transfers between devices, on_device(): dnorm = lax.all_gather(norm_share, ('segment', 'mp'), axis=2, tiled=True)  75.1 us
    ppermute x12, waiting for transfers between devices, shifted(): return lax.ppermute(block, axis, route)  70.4 us
    psum x1, waiting for transfers between devices, broadcast(): return lax.psum(jnp.where(mine, x, jnp.zeros_like(x)), axis)  49.1 us
  transfers between devices with their start and end apart: 30, of which 29 were waited for; matrix products, arithmetic and copies ran while one was open for 2% of the time, Pallas kernels for 0%

commit v1 on v0

--- a/solution.py
+++ b/solution.py
@@ -53,7 +53,7 @@
 
 
 def reduce_rows(partial_value, pieces, finisher):
-    summed = lax.psum(partial_value, "mp")
+    summed = jnp.sum(lax.all_gather(partial_value, "mp"), axis=0)
     return finisher(pieces, summed)
 
 

time: 2380 us -> 1630 us (0.68)
  waiting for transfers between devices: 1670 us -> 1090 us
  blocking collectives: 518 us -> 253 us
  other arithmetic: 53.3 us -> 111 us
  local copies, waits for them, and re-layouts: 20.1 us -> 46.2 us
    psum x13 -> x0, waiting for transfers between devices: 1420 us -> none  [reduce_rows(): summed = lax.psum(partial_value, 'mp')]
    all_gather x0 -> x13, waiting for transfers between devices: none -> 716 us  [reduce_rows(): summed = jnp.sum(lax.all_gather(partial_value, 'mp'), axis=0)]
    psum x2 -> x1, blocking collectives: 393 us -> 127 us  [on_device(): lax.psum((jnp.sum(jnp.exp(logits - peak[..., None]), axis=-1), target_loc...]
    reduce_scatter x0 -> x1, waiting for transfers between devices: none -> 129 us  [on_device(): lax.psum_scatter(norm_part, ('segment', 'mp'), scatter_dimension=2, tiled...]
    reduce_sum x0 -> x13, other arithmetic: none -> 64.7 us  [reduce_rows(): summed = jnp.sum(lax.all_gather(partial_value, 'mp'), axis=0)]
    reduce_sum x0 -> x13, local copies, waits for them, and re-layouts: none -> 24.6 us  [reduce_rows(): summed = jnp.sum(lax.all_gather(partial_value, 'mp'), axis=0)]
  transfers between devices with their start and end apart: 30 -> 31, of which waited for: 29 -> 30; matrix products, arithmetic and copies ran while one was open for 2% -> 4% of each run, Pallas kernels for 0% -> 0%
where the time goes in v1:
time: 1630 us; the launch traced here: 1620 us
  waiting for transfers between devices  1090 us (67%)
  blocking collectives  253 us (16%)
  other arithmetic  111 us (7%)
  matrix products  74.2 us (5%)
  local copies, waits for them, and re-layouts  46.2 us (3%)
  starting transfers between devices  31.5 us (2%)
  between operations  16.9 us (1%)
    all_gather x13, waiting for transfers between devices, reduce_rows(): summed = jnp.sum(lax.all_gather(partial_value, 'mp'), axis=0)  716 us
    reduce_scatter x1, waiting for transfers between devices, on_device(): lax.psum_scatter(norm_part, ('segment', 'mp'), scatter_dimension=2, tiled...  129 us
    psum x1, blocking collectives, on_device(): lax.psum((jnp.sum(jnp.exp(logits - peak[..., None]), axis=-1), target_loc...  127 us
    pmax x1, blocking collectives, on_device(): peak = lax.pmax(local_peak, ('segment', 'mp'))  125 us
    all_gather x1, waiting for transfers between devices, on_device(): dnorm = lax.all_gather(norm_share, ('segment', 'mp'), axis=2, tiled=True)  75.3 us
    ppermute x12, waiting for transfers between devices, shifted(): return lax.ppermute(block, axis, route)  73.1 us
    reduce_sum x13, other arithmetic, reduce_rows(): summed = jnp.sum(lax.all_gather(partial_value, 'mp'), axis=0)  64.7 us
    psum x1, waiting for transfers between devices, broadcast(): return lax.psum(jnp.where(mine, x, jnp.zeros_like(x)), axis)  48.1 us
  transfers between devices with their start and end apart: 31, of which 30 were waited for; matrix products, arithmetic and copies ran while one was open for 4% of the time, Pallas kernels for 0%

profile of v1, /device:TPU:1, one launch (start us, length us, event | category | flops | bytes accessed | tf_op | source)
XLA Modules:
  0.0 1623.8 jit_solution(290381342621903216)
XLA Ops:
  7.2 2.2 fusion.575
  11.3 60.2 %all-gather.30.cloned.1.call-done = f32[2048,1024]{1,0:T(8,128)} async-done(((f32[128,1024]{1,0:T(8,128)}), f32[2048,1024]{1,0:T(8,128)}) %all-gather.30.cloned.1.call-update) | async-done | bytes 8388624 | tf_op jit(solution)/shard_map/all_gather | solution.py:56
  71.5 4.2 reduce_sum.382
  76.9 3.8 collective-permute-start
  82.7 3.0 collective-permute-done
  87.7 2.4 fusion.33
  93.2 53.4 %all-gather.32.cloned.1.call-done = f32[2048,1024]{1,0:T(8,128)} async-done(((f32[128,1024]{1,0:T(8,128)}), f32[2048,1024]{1,0:T(8,128)}) %all-gather.32.cloned.1.call-update) | async-done | bytes 8388624 | tf_op jit(solution)/shard_map/all_gather | solution.py:56
  146.6 5.1 reduce_sum.385
  155.7 3.1 collective-permute-start.1
  160.6 3.9 collective-permute-done.1
  168.0 56.3 %all-gather.34.cloned.1.call-done = f32[2048,1024]{1,0:T(8,128)} async-done(((f32[128,1024]{1,0:T(8,128)}), f32[2048,1024]{1,0:T(8,128)}) %all-gather.34.cloned.1.call-update) | async-done | bytes 8388624 | tf_op jit(solution)/shard_map/all_gather | solution.py:56
  224.4 5.0 reduce_sum.387
  233.5 3.8 collective-permute-start.2
  238.4 3.9 collective-permute-done.2
  243.3 2.4 fusion.29
  245.8 57.3 %all-gather.36.cloned.1.call-done = f32[2048,1024]{1,0:T(8,128)} async-done(((f32[128,1024]{1,0:T(8,128)}), f32[2048,1024]{1,0:T(8,128)}) %all-gather.36.cloned.1.call-update) | async-done | bytes 8388624 | tf_op jit(solution)/shard_map/all_gather | solution.py:56
  303.1 5.0 reduce_sum.389
  310.1 2.1 fusion.309
  312.2 3.8 collective-permute-start.3
  316.1 5.0 collective-permute-done.3
  322.1 2.4 fusion.27
  324.6 57.3 %all-gather.38.cloned.1.call-done = f32[2048,1024]{1,0:T(8,128)} async-done(((f32[128,1024]{1,0:T(8,128)}), f32[2048,1024]{1,0:T(8,128)}) %all-gather.38.cloned.1.call-update) | async-done | bytes 8388624 | tf_op jit(solution)/shard_map/all_gather | solution.py:56
  381.9 5.0 reduce_sum.391
  391.0 3.8 collective-permute-start.4
  394.8 5.0 collective-permute-done.4
  400.9 2.4 fusion.25
  403.8 56.8 %all-gather.40.cloned.1.call-done = f32[2048,1024]{1,0:T(8,128)} async-done(((f32[128,1024]{1,0:T(8,128)}), f32[2048,1024]{1,0:T(8,128)}) %all-gather.40.cloned.1.call-update) | async-done | bytes 8388624 | tf_op jit(solution)/shard_map/all_gather | solution.py:56
  460.6 5.0 reduce_sum.393
  469.8 3.8 collective-permute-start.5
  473.6 5.0 collective-permute-done.5
  479.7 2.4 fusion.23
  482.1 57.3 %all-gather.42.cloned.1.call-done = f32[2048,1024]{1,0:T(8,128)} async-done(((f32[128,1024]{1,0:T(8,128)}), f32[2048,1024]{1,0:T(8,128)}) %all-gather.42.cloned.1.call-update) | async-done | bytes 8388624 | tf_op jit(solution)/shard_map/all_gather | solution.py:56
  539.4 5.1 reduce_sum.395
  550.3 48.1 %all-reduce.3.cloned.1.call-done = bf16[4,128,1024]{1,2,0:T(8,128)(2,1)} async-done(((bf16[4,128,1024]{1,2,0:T(8,128)(2,1)}), bf16[4,128,1024]{1,2,0:T(8,128)(2,1)}) %all-reduce.3.cloned.1.call-update) | async-done | bytes 1048592 | tf_op jit(solution)/shard_map/psum | solution.py:15
  599.9 2.3 fusion.576
  602.2 125.5 %pmax.7 = f32[4,128]{1,0:T(4,128)S(1)} all-reduce(f32[4,128]{1,0:T(4,128)S(1)} %get-tuple-element.44), channel_id=1, replica_groups=mesh['segment'=4,'mp'=16,'dp'=4] {'segment','mp'}, use_global_device_ids=true, to_apply=%region_17.18 | all-reduce | flops 512 | bytes 4096 | tf_op jit(solution)/shard_map/pmax | solution.py:107
  727.6 2.3 exponential_reduce_fusion
  729.9 127.1 %all-reduce = (f32[4,128]{1,0:T(4,128)S(1)}, f32[4,128]{1,0:T(4,128)S(1)}) all-reduce(f32[4,128]{1,0:T(4,128)S(1)} %get-tuple-element.13, f32[4,128]{1,0:T(4,128)S(1)} %get-tuple-element.12), channel_id=1, replica_groups=mesh['segment'=4,'mp'=16,'dp'=4] {'segment','mp'}, use_global_device_ids=true, to_apply=%region_23.24 | all-reduce | flops 1024 | bytes 8192 | tf_op jit(solution)/shard_map/psum | solution.py:108
  861.4 129.3 %reduce-scatter.5.cloned.1.call-done = f32[4,128,16]{1,2,0:T(8,128)} async-done(((f32[4,128,1024]{1,2,0:T(8,128)}), f32[4,128,16]{1,2,0:T(8,128)}) %reduce-scatter.5.cloned.1.call-update) | async-done | bytes 32784 | tf_op jit(solution)/shard_map/reduce_scatter | solution.py:121
  992.7 75.3 %all-gather.28.cloned.1.call-done = bf16[4,128,1024]{1,2,0:T(8,128)(2,1)} async-done(((bf16[4,128,16]{1,2,0:T(8,128)(2,1)}), bf16[4,128,1024]{1,2,0:T(8,128)(2,1)}) %all-gather.28.cloned.1.call-update) | async-done | bytes 1048592 | tf_op jit(solution)/shard_map/all_gather | solution.py:124
  1073.5 55.0 %all-gather.44.cloned.1.call-done = f32[2048,1024]{1,0:T(8,128)} async-done(((f32[128,1024]{1,0:T(8,128)}), f32[2048,1024]{1,0:T(8,128)}) %all-gather.44.cloned.1.call-update) | async-done | bytes 8388624 | tf_op jit(solution)/shard_map/all_gather | solution.py:56
  1128.6 5.0 reduce_sum.404
  1139.5 7.9 collective-permute-done.6
  1150.0 55.4 %all-gather.46.cloned.1.call-done = f32[2048,1024]{1,0:T(8,128)} async-done(((f32[128,1024]{1,0:T(8,128)}), f32[2048,1024]{1,0:T(8,128)}) %all-gather.46.cloned.1.call-update) | async-done | bytes 8388624 | tf_op jit(solution)/shard_map/all_gather | solution.py:56
  1205.4 5.0 reduce_sum.407
  1216.7 7.7 collective-permute-done.7
  1228.6 55.4 %all-gather.48.cloned.1.call-done = f32[2048,1024]{1,0:T(8,128)} async-done(((f32[128,1024]{1,0:T(8,128)}), f32[2048,1024]{1,0:T(8,128)}) %all-gather.48.cloned.1.call-update) | async-done | bytes 8388624 | tf_op jit(solution)/shard_map/all_gather | solution.py:56
  1284.0 5.0 reduce_sum.410
  1295.2 7.9 collective-permute-done.8
  1307.3 55.4 %all-gather.50.cloned.1.call-done = f32[2048,1024]{1,0:T(8,128)} async-done(((f32[128,1024]{1,0:T(8,128)}), f32[2048,1024]{1,0:T(8,128)}) %all-gather.50.cloned.1.call-update) | async-done | bytes 8388624 | tf_op jit(solution)/shard_map/all_gather | solution.py:56
  1362.7 5.0 reduce_sum.413
  1373.9 7.9 collective-permute-done.9
  1386.0 55.4 %all-gather.52.cloned.1.call-done = f32[2048,1024]{1,0:T(8,128)} async-done(((f32[128,1024]{1,0:T(8,128)}), f32[2048,1024]{1,0:T(8,128)}) %all-gather.52.cloned.1.call-update) | async-done | bytes 8388624 | tf_op jit(solution)/shard_map/all_gather | solution.py:56
  1441.4 5.0 reduce_sum.416
  1452.6 7.9 collective-permute-done.10
  1464.7 2.6 convolution_bitcast_fusion
  1467.7 2.9 fusion.406
  1479.7 40.4 %all-gather.54.cloned.1.call-done = f32[2048,1024]{1,0:T(8,128)} async-done(((f32[128,1024]{1,0:T(8,128)}), f32[2048,1024]{1,0:T(8,128)}) %all-gather.54.cloned.1.call-update) | async-done | bytes 8388624 | tf_op jit(solution)/shard_map/all_gather | solution.py:56
  1520.1 5.0 reduce_sum.419
  1531.3 8.0 collective-permute-done.11
  1540.0 6.5 multiply_add_fusion
  1557.8 8.1 multiply_add_fusion.1
  1566.6 14.0 reduce-scatter.9.cloned.1.call-done
  1580.6 35.3 %reduce-scatter.7.cloned.1.call-done = f32[256,512]{1,0:T(8,128)} async-done(((f32[1024,512]{1,0:T(8,128)}), f32[256,512]{1,0:T(8,128)}) %reduce-scatter.7.cloned.1.call-update) | async-done | bytes 524304 | tf_op jit(solution)/shard_map/reduce_scatter | solution.py:154
  (295 shorter events, 135.9 us)
Async XLA Ops:
  7.2 64.3 %all-gather.30.cloned.1.call-start = ((), (), s32[]{:S(2)}) async-start(), calls=%async_computation.10 | async-start | bytes 8912896 | tf_op jit(solution)/shard_map/all_gather | solution.py:56
  11.2 135.3 %all-gather.32.cloned.1.call-start = ((), (), s32[]{:S(2)}) async-start(), calls=%async_computation.11 | async-start | bytes 8912896 | tf_op jit(solution)/shard_map/all_gather | solution.py:56
  76.0 6.5 copy-start.7
  76.9 8.9 collective-permute-start
  90.1 134.3 %all-gather.34.cloned.1.call-start = ((), (), s32[]{:S(2)}) async-start(), calls=%async_computation.12 | async-start | bytes 8912896 | tf_op jit(solution)/shard_map/all_gather | solution.py:56
  146.6 7.1 copy-start.10
  155.7 8.9 collective-permute-start.1
  168.0 135.1 %all-gather.36.cloned.1.call-start = ((), (), s32[]{:S(2)}) async-start(), calls=%async_computation.13 | async-start | bytes 8912896 | tf_op jit(solution)/shard_map/all_gather | solution.py:56
  233.5 8.8 collective-permute-start.2
  245.7 136.2 %all-gather.38.cloned.1.call-start = ((), (), s32[]{:S(2)}) async-start(), calls=%async_computation.14 | async-start | bytes 8912896 | tf_op jit(solution)/shard_map/all_gather | solution.py:56
  312.2 8.9 collective-permute-start.3
  324.5 136.1 %all-gather.40.cloned.1.call-start = ((), (), s32[]{:S(2)}) async-start(), calls=%async_computation.15 | async-start | bytes 8912896 | tf_op jit(solution)/shard_map/all_gather | solution.py:56
  391.0 8.9 collective-permute-start.4
  403.3 136.2 %all-gather.42.cloned.1.call-start = ((), (), s32[]{:S(2)}) async-start(), calls=%async_computation.16 | async-start | bytes 8912896 | tf_op jit(solution)/shard_map/all_gather | solution.py:56
  469.8 8.9 collective-permute-start.5
  482.1 116.3 %all-reduce.3.cloned.1.call-start = ((), (), s32[]{:S(2)}) async-start(), calls=%async_computation.4 | async-start | bytes 2097152 | tf_op jit(solution)/shard_map/psum | solution.py:15
  539.4 7.1 copy-start.15
  548.5 51.4 %copy-start.47 = (bf16[1024,160]{0,1:T(8,128)(2,1)S(1)}, bf16[1024,160]{0,1:T(8,128)(2,1)}, u32[]{:S(2)}) copy-start(bf16[1024,160]{0,1:T(8,128)(2,1)} %param.11) | copy-start | bytes 983044
  549.5 178.1 %copy-start.62 = (s32[4,512]{1,0:T(4,128)S(1)}, s32[4,512]{1,0:T(4,128)}, u32[]{:S(2)}) copy-start(s32[4,512]{1,0:T(4,128)} %param.8) | copy-start | bytes 24580
  549.6 441.2 %reduce-scatter.5.cloned.1.call-start = ((), (), s32[]{:S(2)}) async-start(), calls=%async_computation.5 | async-start | bytes 2129920 | tf_op jit(solution)/shard_map/reduce_scatter | solution.py:121
  861.4 206.6 %all-gather.28.cloned.1.call-start = ((), (), s32[]{:S(2)}) async-start(), calls=%async_computation.6 | async-start | bytes 1064960 | tf_op jit(solution)/shard_map/all_gather | solution.py:124
  992.1 136.4 %all-gather.44.cloned.1.call-start = ((), (), s32[]{:S(2)}) async-start(), calls=%async_computation.17 | async-start | bytes 8912896 | tf_op jit(solution)/shard_map/all_gather | solution.py:56
  992.3 145.4 %copy-start.54 = (f32[128]{0:T(128)}, f32[128]{0:T(128)S(1)}, u32[]{:S(2)}) copy-start(f32[128]{0:T(128)S(1)} %add_rsqrt_fusion.7) | copy-start | bytes 1540
  992.7 77.9 %copy-start.36 = (f32[128,512]{1,0:T(8,128)}, f32[128,512]{1,0:T(8,128)S(1)}, u32[]{:S(2)}) copy-start(f32[128,512]{1,0:T(8,128)S(1)} %fusion.61) | copy-start | bytes 786436
  1073.5 131.9 %all-gather.46.cloned.1.call-start = ((), (), s32[]{:S(2)}) async-start(), calls=%async_computation.18 | async-start | bytes 8912896 | tf_op jit(solution)/shard_map/all_gather | solution.py:56
  1137.9 9.5 collective-permute-start.6
  1139.5 7.9 copy-start.26
  1150.0 134.0 %all-gather.48.cloned.1.call-start = ((), (), s32[]{:S(2)}) async-start(), calls=%async_computation.19 | async-start | bytes 8912896 | tf_op jit(solution)/shard_map/all_gather | solution.py:56
  1212.4 3.9 copy-start.61
  1214.8 9.5 collective-permute-start.7
  1216.7 9.9 copy-start.28
  1228.6 134.1 %all-gather.50.cloned.1.call-start = ((), (), s32[]{:S(2)}) async-start(), calls=%async_computation.20 | async-start | bytes 8912896 | tf_op jit(solution)/shard_map/all_gather | solution.py:56
  1291.1 3.8 copy-start.60
  1293.5 9.5 collective-permute-start.8
  1294.8 76.1 %copy-start.50 = (f32[128]{0:T(128)}, f32[128]{0:T(128)S(1)}, u32[]{:S(2)}) copy-start(f32[128]{0:T(128)S(1)} %add_rsqrt_fusion.4) | copy-start | bytes 1540
  1295.2 10.1 copy-start.30
  1307.3 134.1 %all-gather.52.cloned.1.call-start = ((), (), s32[]{:S(2)}) async-start(), calls=%async_computation.21 | async-start | bytes 8912896 | tf_op jit(solution)/shard_map/all_gather | solution.py:56
  1369.7 3.8 copy-start.59
  1372.2 9.5 collective-permute-start.9
  1373.5 76.1 %copy-start.52 = (f32[128]{0:T(128)}, f32[128]{0:T(128)S(1)}, u32[]{:S(2)}) copy-start(f32[128]{0:T(128)S(1)} %add_rsqrt_fusion.3) | copy-start | bytes 1540
  1373.9 10.1 copy-start.32
  1386.0 134.1 %all-gather.54.cloned.1.call-start = ((), (), s32[]{:S(2)}) async-start(), calls=%async_computation.22 | async-start | bytes 8912896 | tf_op jit(solution)/shard_map/all_gather | solution.py:56
  1448.4 3.8 copy-start.58
  1450.9 9.5 collective-permute-start.10
  1452.6 10.1 copy-start.34
  1464.6 101.9 %reduce-scatter.11.cloned.1.call-start = ((), (), s32[]{:S(2)}) async-start(), calls=%async_computation.9 | async-start | bytes 819200 | tf_op jit(solution)/shard_map/reduce_scatter | solution.py:156
  1467.4 113.2 %reduce-scatter.9.cloned.1.call-start = ((), (), s32[]{:S(2)}) async-start(), calls=%async_computation.8 | async-start | bytes 2621440 | tf_op jit(solution)/shard_map/reduce_scatter | solution.py:155
  1467.6 4.8 copy-start.17
  1467.7 4.8 copy-start.29
  1470.6 3.6 copy-start.19
  1470.6 3.6 copy-start.31
  1472.4 3.6 copy-start.21
  1472.4 3.6 copy-start.33
  1474.3 3.6 copy-start.23
  1474.3 3.6 copy-start.35
  1527.1 12.9 copy-start.5
  1529.7 9.6 collective-permute-start.11
  1531.0 8.3 copy-start.56
  1546.6 69.3 %reduce-scatter.7.cloned.1.call-start = ((), (), s32[]{:S(2)}) async-start(), calls=%async_computation.7 | async-start | bytes 2621440 | tf_op jit(solution)/shard_map/reduce_scatter | solution.py:154
  1547.2 3.5 copy-start.40
  1550.7 3.5 copy-start.44
  1550.7 3.5 copy-start.53
  1552.5 3.6 copy-start.46
  1554.2 3.6 copy-start.57
  (30 other events, 41.6 us)
Sparse Core Ops, SparseCore 0:
  11.4 60.1 all-gather.29
  90.2 56.3 all-gather.31
  168.1 56.2 all-gather.33
  245.8 57.2 all-gather.35
  324.6 57.1 all-gather.37
  403.4 57.1 all-gather.39
  482.2 57.2 all-gather.41
  549.7 48.6 all-reduce.2
  861.5 129.1 reduce-scatter.4
  993.7 74.2 all-gather.27
  1073.6 54.9 all-gather.43
  1150.1 55.2 all-gather.45
  1228.7 55.2 all-gather.47
  1307.4 55.2 all-gather.49
  1386.1 55.2 all-gather.51
  1464.8 55.2 all-gather.53
  1523.0 20.8 reduce-scatter.10
  1546.9 33.6 reduce-scatter.8
  1583.9 31.9 reduce-scatter.6
